TPU v7x, 256 devices: a whole 4x4x8 slice. The times are simulated.
256 devices in a mesh: rows: 32 (over x, z_lo, core), cols: 8 (over y, z_hi).
Axes of the slice: x: 4, y: 4, z: 8 (z_hi: 2, z_lo: 4; z = z_hi * 4 + z_lo), core: 2. Of those that a mesh axis runs over, the one named last changes fastest.
Arguments:
- matrix_blocks: bfloat16 [8192, 64, 1728], P(('rows', 'cols')), may hold values from -0.75 to 0.75
- restrict: bfloat16 [8192, 4096], P(('rows', 'cols')), may hold values from -1.5 to 1.5
- columns: int32 [8192, 27], P(('rows', 'cols')), may hold values from 0 to 767
- counts: int32 [8192], P(('rows', 'cols')), may hold values from 8 to 27, as said below
- aggregate: int32 [8192], P(('rows', 'cols')), may hold values from 0 to 1
Outputs:
- coarse: float32 [512, 64, 3072], P(('rows', 'cols'))
Inputs may be any that keep to these rules, and one draw needn't show every extreme that they name: `counts`: used slots are the first ones of a row; some row uses all 27.
All inputs are finite; a program needn't handle non-finite values.
Results may differ from a plain program's by a relative error of at most 0.0029.
Values may be sent and summed in bfloat16 or wider, within the bound.
A program may use at most 192 MiB of HBM per device.

v0:
```python
import jax
import jax.numpy as jnp
from jax import lax
from jax.sharding import PartitionSpec as P

BLK = 64
SLOTS = 27
ROWS_DEV = 32
AGG_DEV = 2


def padded(block, sides, width):
    for axis, dim in sides:
        count = lax.axis_size(axis)
        forward = [(i, i + 1) for i in range(count - 1)]
        backward = [(target, source) for source, target in forward]
        low = lax.ppermute(
            lax.slice_in_dim(block, block.shape[dim] - width, None, axis=dim), axis, forward
        )
        high = lax.ppermute(lax.slice_in_dim(block, 0, width, axis=dim), axis, backward)
        block = jnp.concatenate([low, block, high], axis=dim)
    return block


def per_device(matrix_blocks, restrict, columns, counts, aggregate):
    col_count = lax.axis_size("cols")
    row_count = lax.axis_size("rows")
    slab_index = lax.axis_index("rows")
    slab_rows = ROWS_DEV * col_count
    window = 3 * AGG_DEV * col_count
    slab_blocks, slab_aggs = (
        lax.all_gather(restrict, "cols", axis=0, tiled=True),
        lax.all_gather(aggregate, "cols", axis=0, tiled=True),
    )
    near_blocks, near_aggs = (
        padded(slab_blocks, (("rows", 0),), slab_rows),
        padded(slab_aggs, (("rows", 0),), slab_rows),
    )
    slot_index = jnp.arange(SLOTS, dtype=jnp.int32)
    inside = ((columns >= slab_rows) | (slab_index > 0)) & (
        (columns < 2 * slab_rows) | (slab_index < row_count - 1)
    )
    live_mask = ((slot_index[None, :] < counts[:, None]) & inside).astype(jnp.float32)
    slot_ids = columns // ROWS_DEV * AGG_DEV + near_aggs[columns]
    segment = aggregate[:, None] * window + slot_ids
    targets = jnp.arange(AGG_DEV * window, dtype=jnp.int32)
    one_hot = (segment[:, :, None] == targets[None, None, :]).astype(jnp.float32) * live_mask[
        :, :, None
    ]
    own_blocks = restrict.reshape(ROWS_DEV, BLK, BLK)
    left_prod = jnp.einsum(
        "ips,isn->ipn", own_blocks, matrix_blocks, preferred_element_type=jnp.float32
    )
    left_prod = left_prod.astype(jnp.bfloat16).reshape(ROWS_DEV, BLK, SLOTS, BLK)
    far_blocks = near_blocks[columns.reshape(-1)].reshape(ROWS_DEV, SLOTS, BLK, BLK)
    products = jnp.einsum(
        "ipks,ikqs->ikpq", left_prod, far_blocks, preferred_element_type=jnp.float32
    )
    summed = jnp.einsum(
        "ikm,ikpq->mpq",
        one_hot,
        products,
        precision=lax.Precision.HIGHEST,
        preferred_element_type=jnp.float32,
    )
    return (
        summed.reshape(AGG_DEV, window, BLK, BLK)
        .transpose(0, 2, 1, 3)
        .reshape(AGG_DEV, BLK, window * BLK)
    )


def solution(mesh):
    return jax.shard_map(
        per_device,
        mesh=mesh,
        in_specs=(
            P(("rows", "cols"), None, None),
            P(("rows", "cols"), None),
            P(("rows", "cols"), None),
            P(("rows", "cols")),
            P(("rows", "cols")),
        ),
        out_specs=P(("rows", "cols"), None, None),
        check_vma=False,
    )
```

profile of v0, /device:TPU:97, one launch (start us, length us, event | category | flops | bytes accessed | tf_op | source)
XLA Modules:
  0.0 337.9 jit_solution(14347546717908960223)
XLA Ops:
  6.5 0.0 all-gather.2.cloned.1.call-start
  6.5 0.7 all-gather.2.cloned.1.call-update
  7.3 74.1 %all-gather.2.cloned.1.call-done = bf16[256,4096]{1,0:T(8,128)(2,1)} async-done(((bf16[32,4096]{1,0:T(8,128)(2,1)}), bf16[256,4096]{1,0:T(8,128)(2,1)}) %all-gather.2.cloned.1.call-update) | async-done | bytes 2097168 | tf_op jit(solution)/shard_map/all_gather | solution.py:32
  81.3 6.3 %collective-permute-start.3 = (bf16[256,4096]{1,0:T(8,128)(2,1)}, bf16[256,4096]{1,0:T(8,128)(2,1)}, u32[]{:S(2)}, u32[]{:S(2)}) collective-permute-start(bf16[256,4096]{1,0:T(8,128)(2,1)} %all-gather.2.cloned.1.call-done), channel_id=1, source_target_pairs={{8,0},{16,8},{24,16},{32,24},{40,32},{48,40},{56,48},{64,56},{72,6... | collective-permute-start | bytes 6291464 | tf_op jit(solution)/shard_map/ppermute | solution.py:20
  87.6 5.5 %collective-permute-start.2 = (bf16[256,4096]{1,0:T(8,128)(2,1)}, bf16[256,4096]{1,0:T(8,128)(2,1)}, u32[]{:S(2)}, u32[]{:S(2)}) collective-permute-start(bf16[256,4096]{1,0:T(8,128)(2,1)} %all-gather.2.cloned.1.call-done), channel_id=1, source_target_pairs={{0,8},{8,16},{16,24},{24,32},{32,40},{40,48},{48,56},{56,64},{64,7... | collective-permute-start | bytes 6291464 | tf_op jit(solution)/shard_map/ppermute | solution.py:17
  93.2 1.3 dynamic-slice
  95.1 0.9 dynamic-update-slice
  95.9 44.7 %all-reduce = s32[256]{0:T(256)S(1)} all-reduce(s32[256]{0:T(256)S(1)} %dynamic-update-slice), channel_id=1, replica_groups=mesh['rows'=32,'cols'=8] {'cols'}, use_global_device_ids=true, to_apply=%add | all-reduce | flops 256 | bytes 2048
  140.6 1.9 collective-permute-start.1
  142.5 6.3 %collective-permute-start = (s32[256]{0:T(256)S(1)}, s32[256]{0:T(256)S(1)}, u32[]{:S(2)}, u32[]{:S(2)}) collective-permute-start(s32[256]{0:T(256)S(1)} %all-reduce), channel_id=1, source_target_pairs={{0,8},{8,16},{16,24},{24,32},{32,40},{40,48},{48,56},{56,64},{64,7... | collective-permute-start | bytes 3080 | tf_op jit(solution)/shard_map/ppermute | solution.py:17
  148.9 1.5 reshape.51
  150.4 0.8 reshape.53
  151.2 0.7 add_select_fusion
  151.9 0.1 reshape.59
  152.1 0.7 broadcast_multiply_fusion
  152.7 0.8 fusion.18
  153.5 8.1 %convolution_convert_fusion = bf16[32,64,1728]{2,1,0:T(8,128)(2,1)} fusion(bf16[32,64,64]{2,1,0:T(8,128)(2,1)S(1)} %reshape.51, bf16[32,64,1728]{2,1,0:T(8,128)(2,1)} %param.5), kind=kOutput, calls=%fused_computation.7 | convolution fusion | flops 456523776 | bytes 14417920 | tf_op jit(solution)/shard_map/ips,isn->ipn/dot_general | solution.py:51
  161.6 22.9 %reshape.52 = bf16[32,64,27,64]{3,2,1,0:T(8,128)(2,1)} reshape(bf16[32,64,1728]{2,1,0:T(8,128)(2,1)} %convolution_convert_fusion) | data formatting | bytes 14155776 | tf_op jit(solution)/shard_map/reshape | solution.py:54
  184.5 0.1 copy.13
  184.6 0.0 collective-permute-done.1
  184.6 0.0 collective-permute-done
  184.6 0.0 copy-start.1
  184.6 0.0 copy-start
  184.7 3.7 %gather_fusion = s32[864]{0:T(1024)S(1)} fusion(s32[768]{0:T(1024)S(1)} %pad_add_fusion, s32[1024]{0:T(1024)S(1)} %pad_clamp_fusion.1), kind=kCustom, calls=%fused_computation | custom fusion | bytes 10368 | tf_op jit(solution)/shard_map/gather | solution.py:44
  188.3 0.1 reshape.58
  188.4 0.0 copy-done.1
  188.4 0.1 fusion.15
  188.5 0.1 copy.12
  188.6 0.0 collective-permute-done.3
  188.6 0.0 collective-permute-done.2
  188.6 0.0 copy-done
  188.6 5.5 %pad_maximum_fusion = bf16[768,4096]{1,0:T(8,128)(2,1)} fusion(bf16[256,4096]{1,0:T(8,128)(2,1)} %collective-permute-done.3, bf16[256,4096]{1,0:T(8,128)(2,1)S(1)} %copy-done, bf16[256,4096]{1,0:T(8,128)(2,1)} %collective-permute-done.2), kind=kLoop, calls=%fused_computation.6 | loop fusion | flops 18874368 | bytes 12582912 | tf_op jit(solution)/shard_map/concatenate | solution.py:21
  194.1 18.5 %gather_fusion.1 = bf16[864,4096]{1,0:T(8,128)(2,1)} fusion(bf16[768,4096]{1,0:T(8,128)(2,1)} %pad_maximum_fusion, s32[1024]{0:T(1024)S(1)} %pad_clamp_fusion), kind=kCustom, calls=%fused_computation.1 | custom fusion | bytes 14159232 | tf_op jit(solution)/shard_map/gather | solution.py:55
  212.6 20.0 %reshape.54 = bf16[32,27,64,64]{3,2,1,0:T(8,128)(2,1)} reshape(bf16[864,4096]{1,0:T(8,128)(2,1)} %gather_fusion.1) | data formatting | bytes 14155776 | tf_op jit(solution)/shard_map/reshape | solution.py:55
  232.5 23.6 %fusion.2 = f32[32,27,64,64]{3,2,1,0:T(8,128)} fusion(bf16[32,27,64,64]{3,2,1,0:T(8,128)(2,1)} %reshape.54, bf16[32,64,27,64]{3,2,1,0:T(8,128)(2,1)} %reshape.52), kind=kOutput, calls=%fused_computation.4 | convolution fusion | flops 452984832 | bytes 28311552 | tf_op jit(solution)/shard_map/ipks,ikqs->ikpq/dot_general | solution.py:56
  256.1 64.2 %fusion.4 = f32[96,64,64]{0,2,1:T(8,128)} fusion(f32[32,27,64,64]{3,2,1,0:T(8,128)} %fusion.2, f32[32,27]{0,1:T(8,128)S(1)} %copy.13, s32[32,27]{0,1:T(8,128)S(1)} %copy.12), kind=kOutput, calls=%fused_computation.8 | convolution fusion | flops 4077029376 | bytes 15735552 | tf_op jit(solution)/shard_map/ikm,ikpq->mpq/dot_general | solution.py:59
  320.3 4.0 %copy.16 = f32[96,64,64]{2,1,0:T(8,128)S(1)} copy(f32[96,64,64]{0,2,1:T(8,128)} %fusion.4) | data formatting | bytes 3145728 | tf_op jit(solution)/shard_map/ikm,ikpq->mpq/dot_general | solution.py:59
  324.3 3.5 %copy.17 = f32[2,64,48,64]{3,2,1,0:T(8,128)} copy(f32[2,64,48,64]{3,1,2,0:T(8,128)S(1)} %bitcast.15) | data formatting | bytes 3145728 | tf_op jit(solution)/shard_map/transpose | solution.py:68
  327.8 3.2 reshape.56
  (5 shorter events, 0.0 us)
Async XLA Ops:
  6.5 74.8 %all-gather.2.cloned.1.call-start = ((), (), s32[]{:S(2)}) async-start(), calls=%async_computation | async-start | bytes 2359296 | tf_op jit(solution)/shard_map/all_gather | solution.py:32
  81.3 107.3 %collective-permute-start.3 = (bf16[256,4096]{1,0:T(8,128)(2,1)}, bf16[256,4096]{1,0:T(8,128)(2,1)}, u32[]{:S(2)}, u32[]{:S(2)}) collective-permute-start(bf16[256,4096]{1,0:T(8,128)(2,1)} %all-gather.2.cloned.1.call-done), channel_id=1, source_target_pairs={{8,0},{16,8},{24,16},{32,24},{40,32},{48,40},{56,48},{64,56},{72,6... | collective-permute-start | bytes 6291464 | tf_op jit(solution)/shard_map/ppermute | solution.py:20
  87.6 101.0 %collective-permute-start.2 = (bf16[256,4096]{1,0:T(8,128)(2,1)}, bf16[256,4096]{1,0:T(8,128)(2,1)}, u32[]{:S(2)}, u32[]{:S(2)}) collective-permute-start(bf16[256,4096]{1,0:T(8,128)(2,1)} %all-gather.2.cloned.1.call-done), channel_id=1, source_target_pairs={{0,8},{8,16},{16,24},{24,32},{32,40},{40,48},{48,56},{56,64},{64,7... | collective-permute-start | bytes 6291464 | tf_op jit(solution)/shard_map/ppermute | solution.py:17
  140.6 44.0 %collective-permute-start.1 = (s32[256]{0:T(256)S(1)}, s32[256]{0:T(256)S(1)}, u32[]{:S(2)}, u32[]{:S(2)}) collective-permute-start(s32[256]{0:T(256)S(1)} %all-reduce), channel_id=1, source_target_pairs={{8,0},{16,8},{24,16},{32,24},{40,32},{48,40},{56,48},{64,56},{72,6... | collective-permute-start | bytes 3080 | tf_op jit(solution)/shard_map/ppermute | solution.py:20
  142.5 42.1 %collective-permute-start = (s32[256]{0:T(256)S(1)}, s32[256]{0:T(256)S(1)}, u32[]{:S(2)}, u32[]{:S(2)}) collective-permute-start(s32[256]{0:T(256)S(1)} %all-reduce), channel_id=1, source_target_pairs={{0,8},{8,16},{16,24},{24,32},{32,40},{40,48},{48,56},{56,64},{64,7... | collective-permute-start | bytes 3080 | tf_op jit(solution)/shard_map/ppermute | solution.py:17
  184.6 3.8 %copy-start.1 = (s32[32,27]{1,0:T(8,128)S(1)}, s32[32,27]{1,0:T(8,128)}, u32[]{:S(2)}) copy-start(s32[32,27]{1,0:T(8,128)} %param.7) | copy-start | bytes 10372
  184.6 4.0 %copy-start = (bf16[256,4096]{1,0:T(8,128)(2,1)S(1)}, bf16[256,4096]{1,0:T(8,128)(2,1)}, u32[]{:S(2)}) copy-start(bf16[256,4096]{1,0:T(8,128)(2,1)} %all-gather.2.cloned.1.call-done) | copy-start | bytes 6291460
Sparse Core Ops, SparseCore 0:
  10.0 71.3 all-gather.1
where the time goes:
time: 339 us; the launch traced here: 338 us
  matrix products  95.9 us (28%)
  local copies, waits for them, and re-layouts  80.5 us (24%)
  waiting for transfers between devices  74.8 us (22%)
  blocking collectives  44.7 us (13%)
  starting transfers between devices  20.1 us (6%)
  between operations  14.2 us (4%)
  other arithmetic  7.74 us (2%)
    all_gather x1, waiting for transfers between devices, per_device(): lax.all_gather(restrict, 'cols', axis=0, tiled=True)  74.1 us
    dot_general x1, matrix products, per_device(): jnp.einsum('ikm,ikpq->mpq', one_hot, products, precision=lax.Precision.HI...  64.2 us
    unnamed x1, blocking collectives  44.7 us
    dot_general x1, matrix products, per_device(): jnp.einsum('ipks,ikqs->ikpq', left_prod, far_blocks, preferred_element_ty...  23.6 us
    reshape x1, local copies, waits for them, and re-layouts, per_device(): left_prod.astype(jnp.bfloat16).reshape(ROWS_DEV, BLK, SLOTS, BLK)  22.9 us
    reshape x1, local copies, waits for them, and re-layouts, per_device(): near_blocks[columns.reshape(-1)].reshape(ROWS_DEV, SLOTS, BLK, BLK)  20 us
    gather x1, local copies, waits for them, and re-layouts, per_device(): near_blocks[columns.reshape(-1)].reshape(ROWS_DEV, SLOTS, BLK, BLK)  18.5 us
    ppermute x2, starting transfers between devices, padded(): lax.ppermute(lax.slice_in_dim(block, block.shape[dim] - width, None, axis...  11.8 us
  transfers between devices with their start and end apart: 5, of which 1 were waited for; matrix products, arithmetic and copies ran while one was open for 12% of the time, Pallas kernels for 0%

commit v1 on v0

--- a/solution.py
+++ b/solution.py
@@ -7,6 +7,13 @@
 SLOTS = 27
 ROWS_DEV = 32
 AGG_DEV = 2
+
+
+def exchange_gather(shard, axis, dim):
+    n_dev = lax.axis_size(axis)
+    tiles = jnp.stack([shard for _ in range(n_dev)])
+    tiles = lax.all_to_all(tiles, axis, split_axis=0, concat_axis=0)
+    return jnp.concatenate(tiles, axis=dim)
 
 
 def padded(block, sides, width):
@@ -29,7 +36,7 @@
     slab_rows = ROWS_DEV * col_count
     window = 3 * AGG_DEV * col_count
     slab_blocks, slab_aggs = (
-        lax.all_gather(restrict, "cols", axis=0, tiled=True),
+        exchange_gather(restrict, "cols", 0),
         lax.all_gather(aggregate, "cols", axis=0, tiled=True),
     )
     near_blocks, near_aggs = (

time: 339 us -> 305 us (0.90)
  the two profiles are of different devices: /device:TPU:97 before, /device:TPU:229 now
where the time goes in v1:
time: 305 us; the launch traced here: 304 us
  matrix products  95.9 us (31%)
  blocking collectives  93.5 us (31%)
  local copies, waits for them, and re-layouts  81 us (27%)
  starting transfers between devices  26.9 us (9%)
  other arithmetic  5.66 us (2%)
    dot_general x1, matrix products, per_device(): jnp.einsum('ikm,ikpq->mpq', one_hot, products, precision=lax.Precision.HI...  64.2 us
    unnamed x1, blocking collectives  54 us
    all_to_all x1, blocking collectives, exchange_gather(): tiles = lax.all_to_all(tiles, axis, split_axis=0, concat_axis=0)  39.5 us
    dot_general x1, matrix products, per_device(): jnp.einsum('ipks,ikqs->ikpq', left_prod, far_blocks, preferred_element_ty...  23.6 us
    reshape x1, local copies, waits for them, and re-layouts, per_device(): left_prod.astype(jnp.bfloat16).reshape(ROWS_DEV, BLK, SLOTS, BLK)  22.9 us
    reshape x1, local copies, waits for them, and re-layouts, per_device(): near_blocks[columns.reshape(-1)].reshape(ROWS_DEV, SLOTS, BLK, BLK)  20 us
    ppermute x2, starting transfers between devices, padded(): lax.ppermute(lax.slice_in_dim(block, 0, width, axis=dim), axis, backward)  18.7 us
    gather x1, local copies, waits for them, and re-layouts, per_device(): near_blocks[columns.reshape(-1)].reshape(ROWS_DEV, SLOTS, BLK, BLK)  18.5 us
  transfers between devices with their start and end apart: 4, of which 0 were waited for; matrix products, arithmetic and copies ran while one was open for 13% of the time, Pallas kernels for 0%

profile of v1, /device:TPU:229, one launch (start us, length us, event | category | flops | bytes accessed | tf_op | source)
XLA Modules:
  0.0 303.8 jit_solution(14577961655146375104)
XLA Ops:
  0.0 0.0 copy-start.2
  0.0 0.0 copy-start
  0.0 0.0 copy-start.1
  0.0 1.2 stack.2
  1.2 39.5 %all_to_all.5 = bf16[8,32,4096]{2,1,0:T(8,128)(2,1)S(1)} all-to-all(bf16[8,32,4096]{2,1,0:T(8,128)(2,1)S(1)} %stack.2), channel_id=1, replica_groups=mesh['rows'=32,'cols'=8] {'cols'}, dimensions={0} | all-to-all | bytes 4194304 | tf_op jit(solution)/shard_map/all_to_all | solution.py:15
  40.7 16.8 %collective-permute-start.3 = (bf16[256,4096]{1,0:T(8,128)(2,1)S(1)}, bf16[256,4096]{1,0:T(8,128)(2,1)}, u32[]{:S(2)}, u32[]{:S(2)}) collective-permute-start(bf16[256,4096]{1,0:T(8,128)(2,1)S(1)} %bitcast.17), channel_id=1, source_target_pairs={{8,0},{16,8},{24,16},{32,24},{40,32},{48,40},{56,48},{64,56},{72,6... | collective-permute-start | bytes 6291464 | tf_op jit(solution)/shard_map/ppermute | solution.py:27
  57.5 1.9 collective-permute-start.2
  59.4 1.3 dynamic-slice
  61.3 0.9 dynamic-update-slice
  62.2 54.0 %all-reduce = s32[256]{0:T(256)S(1)} all-reduce(s32[256]{0:T(256)S(1)} %dynamic-update-slice), channel_id=1, replica_groups=mesh['rows'=32,'cols'=8] {'cols'}, use_global_device_ids=true, to_apply=%add | all-reduce | flops 256 | bytes 2048
  116.2 1.9 collective-permute-start.1
  118.1 6.3 %collective-permute-start = (s32[256]{0:T(256)S(1)}, s32[256]{0:T(256)S(1)}, u32[]{:S(2)}, u32[]{:S(2)}) collective-permute-start(s32[256]{0:T(256)S(1)} %all-reduce), channel_id=1, source_target_pairs={{0,8},{8,16},{16,24},{24,32},{32,40},{40,48},{48,56},{56,64},{64,7... | collective-permute-start | bytes 3080 | tf_op jit(solution)/shard_map/ppermute | solution.py:24
  124.5 1.5 reshape.56
  125.9 0.0 copy-done
  125.9 0.1 reshape.59
  126.1 0.1 reshape.65
  126.2 0.0 copy-done.2
  126.2 0.0 copy-done.1
  126.2 0.1 fusion.18
  126.3 8.1 %convolution_convert_fusion = bf16[32,64,1728]{2,1,0:T(8,128)(2,1)} fusion(bf16[32,64,64]{2,1,0:T(8,128)(2,1)S(1)} %reshape.56, bf16[32,64,1728]{2,1,0:T(8,128)(2,1)} %param.5), kind=kOutput, calls=%fused_computation.7 | convolution fusion | flops 456523776 | bytes 14417920 | tf_op jit(solution)/shard_map/ips,isn->ipn/dot_general | solution.py:58
  134.4 22.9 %reshape.57 = bf16[32,64,27,64]{3,2,1,0:T(8,128)(2,1)} reshape(bf16[32,64,1728]{2,1,0:T(8,128)(2,1)} %convolution_convert_fusion) | data formatting | bytes 14155776 | tf_op jit(solution)/shard_map/reshape | solution.py:61
  157.4 0.1 copy.13
  157.4 0.0 collective-permute-done.1
  157.4 0.0 collective-permute-done
  157.5 3.7 %gather_fusion = s32[864]{0:T(1024)S(1)} fusion(s32[768]{0:T(1024)S(1)} %pad_add_fusion, s32[1024]{0:T(1024)S(1)} %pad_clamp_fusion.1), kind=kCustom, calls=%fused_computation | custom fusion | bytes 10368 | tf_op jit(solution)/shard_map/gather | solution.py:51
  161.1 0.1 reshape.64
  161.2 0.1 fusion.15
  161.3 0.1 copy.12
  161.4 0.0 collective-permute-done.3
  161.4 0.0 collective-permute-done.2
  161.4 5.5 %pad_maximum_fusion = bf16[768,4096]{1,0:T(8,128)(2,1)} fusion(bf16[256,4096]{1,0:T(8,128)(2,1)} %collective-permute-done.3, bf16[256,4096]{1,0:T(8,128)(2,1)S(1)} %bitcast.19, bf16[256,4096]{1,0:T(8,128)(2,1)} %collective-permute-done.2), kind=kLoop, calls=%fused_computation.6 | loop fusion | flops 18874368 | bytes 12582912 | tf_op jit(solution)/shard_map/concatenate | solution.py:28
  166.9 18.5 %gather_fusion.1 = bf16[864,4096]{1,0:T(8,128)(2,1)} fusion(bf16[768,4096]{1,0:T(8,128)(2,1)} %pad_maximum_fusion, s32[1024]{0:T(1024)S(1)} %pad_clamp_fusion), kind=kCustom, calls=%fused_computation.1 | custom fusion | bytes 14159232 | tf_op jit(solution)/shard_map/gather | solution.py:62
  185.3 20.0 %reshape.60 = bf16[32,27,64,64]{3,2,1,0:T(8,128)(2,1)} reshape(bf16[864,4096]{1,0:T(8,128)(2,1)} %gather_fusion.1) | data formatting | bytes 14155776 | tf_op jit(solution)/shard_map/reshape | solution.py:62
  205.3 23.6 %fusion.2 = f32[32,27,64,64]{3,2,1,0:T(8,128)} fusion(bf16[32,27,64,64]{3,2,1,0:T(8,128)(2,1)} %reshape.60, bf16[32,64,27,64]{3,2,1,0:T(8,128)(2,1)} %reshape.57), kind=kOutput, calls=%fused_computation.4 | convolution fusion | flops 452984832 | bytes 28311552 | tf_op jit(solution)/shard_map/ipks,ikqs->ikpq/dot_general | solution.py:63
  228.9 64.2 %fusion.4 = f32[96,64,64]{0,2,1:T(8,128)} fusion(f32[32,27,64,64]{3,2,1,0:T(8,128)} %fusion.2, f32[32,27]{0,1:T(8,128)S(1)} %copy.13, s32[32,27]{0,1:T(8,128)S(1)} %copy.12), kind=kOutput, calls=%fused_computation.8 | convolution fusion | flops 4077029376 | bytes 15735552 | tf_op jit(solution)/shard_map/ikm,ikpq->mpq/dot_general | solution.py:66
  293.1 4.0 %copy.16 = f32[96,64,64]{2,1,0:T(8,128)S(1)} copy(f32[96,64,64]{0,2,1:T(8,128)} %fusion.4) | data formatting | bytes 3145728 | tf_op jit(solution)/shard_map/ikm,ikpq->mpq/dot_general | solution.py:66
  297.1 3.5 %copy.17 = f32[2,64,48,64]{3,2,1,0:T(8,128)} copy(f32[2,64,48,64]{3,1,2,0:T(8,128)S(1)} %bitcast.16) | data formatting | bytes 3145728 | tf_op jit(solution)/shard_map/transpose | solution.py:75
  300.6 3.2 %reshape.62 = f32[2,64,3072]{2,1,0:T(8,128)} reshape(f32[2,64,48,64]{3,2,1,0:T(8,128)} %copy.17) | data formatting | bytes 3145728 | tf_op jit(solution)/shard_map/reshape | solution.py:76
  (7 shorter events, 0.0 us)
Async XLA Ops:
  0.0 126.2 %copy-start.2 = (s32[32]{0:T(128)S(1)}, s32[32]{0:T(128)}, u32[]{:S(2)}) copy-start(s32[32]{0:T(128)} %param.9) | copy-start | bytes 388
  0.0 125.9 %copy-start = (s32[32,27]{1,0:T(8,128)S(1)}, s32[32,27]{1,0:T(8,128)}, u32[]{:S(2)}) copy-start(s32[32,27]{1,0:T(8,128)} %param.7) | copy-start | bytes 10372
  0.0 126.2 %copy-start.1 = (s32[32]{0:T(128)S(1)}, s32[32]{0:T(128)}, u32[]{:S(2)}) copy-start(s32[32]{0:T(128)} %param.8) | copy-start | bytes 388
  40.7 120.7 %collective-permute-start.3 = (bf16[256,4096]{1,0:T(8,128)(2,1)S(1)}, bf16[256,4096]{1,0:T(8,128)(2,1)}, u32[]{:S(2)}, u32[]{:S(2)}) collective-permute-start(bf16[256,4096]{1,0:T(8,128)(2,1)S(1)} %bitcast.17), channel_id=1, source_target_pairs={{8,0},{16,8},{24,16},{32,24},{40,32},{48,40},{56,48},{64,56},{72,6... | collective-permute-start | bytes 6291464 | tf_op jit(solution)/shard_map/ppermute | solution.py:27
  57.5 103.9 %collective-permute-start.2 = (bf16[256,4096]{1,0:T(8,128)(2,1)S(1)}, bf16[256,4096]{1,0:T(8,128)(2,1)}, u32[]{:S(2)}, u32[]{:S(2)}) collective-permute-start(bf16[256,4096]{1,0:T(8,128)(2,1)S(1)} %bitcast.18), channel_id=1, source_target_pairs={{0,8},{8,16},{16,24},{24,32},{32,40},{40,48},{48,56},{56,64},{64,7... | collective-permute-start | bytes 6291464 | tf_op jit(solution)/shard_map/ppermute | solution.py:24
  116.2 41.3 %collective-permute-start.1 = (s32[256]{0:T(256)S(1)}, s32[256]{0:T(256)S(1)}, u32[]{:S(2)}, u32[]{:S(2)}) collective-permute-start(s32[256]{0:T(256)S(1)} %all-reduce), channel_id=1, source_target_pairs={{8,0},{16,8},{24,16},{32,24},{40,32},{48,40},{56,48},{64,56},{72,6... | collective-permute-start | bytes 3080 | tf_op jit(solution)/shard_map/ppermute | solution.py:27
  118.1 39.3 %collective-permute-start = (s32[256]{0:T(256)S(1)}, s32[256]{0:T(256)S(1)}, u32[]{:S(2)}, u32[]{:S(2)}) collective-permute-start(s32[256]{0:T(256)S(1)} %all-reduce), channel_id=1, source_target_pairs={{0,8},{8,16},{16,24},{24,32},{32,40},{40,48},{48,56},{56,64},{64,7... | collective-permute-start | bytes 3080 | tf_op jit(solution)/shard_map/ppermute | solution.py:24
